TPU v7x, 128 devices: a whole 4x4x4 slice. The times are simulated.
128 devices in a mesh: wake: 16 (over y_hi, x, core), grid: 8 (over z, y_lo).
Axes of the slice: x: 4, y: 4 (y_hi: 2, y_lo: 2; y = y_hi * 2 + y_lo), z: 4, core: 2. Of those that a mesh axis runs over, the one named last changes fastest.
Arguments:
- flow: float32 [5, 256, 131072], P(None, 'wake', 'grid'), may hold values from -6 to 6
- section_map: int32 [256, 131072], P('wake', 'grid'), may hold values from 0 to 2
- viscosity: float32 [3, 5], replicated, may hold values from 0.12 to 0.24
- particle_position: float32 [3, 32768], P(None, ('wake', 'grid')), may hold values from 0 to 1
- particle_strength: float32 [3, 32768], P(None, ('wake', 'grid')), may hold values from -0.6 to 0.6
- particle_core: float32 [32768], P(('wake', 'grid')), may hold values from 0.08 to 0.16
- shed_counts: int32 [16], replicated, may hold values from 512 to 2048, as said below
- node_position: float32 [3, 131072], P(None, ('wake', 'grid')), may hold values from 0 to 1
- node_block: int32 [131072, 1], P(('wake', 'grid')), may hold values from 0 to 15; in each aligned block of 1024 rows (0 to 1023, 1024 to 2047, ...) at most 128 rows name the same one
Outputs:
- flow_out: float32 [5, 256, 131072], P(None, 'wake', 'grid')
- particle_velocity: float32 [3, 32768], P(None, ('wake', 'grid'))
- particle_stretching: float32 [3, 32768], P(None, ('wake', 'grid'))
Inputs may be any that keep to these rules, and one draw needn't show every extreme that they name: `shed_counts`: at least one block holds 2048 live particles. `node_block`: among the 1024 nodes of one device (aligned blocks of nodes), at most 128 name any one block, and some block is named by exactly 128.
All inputs are finite; a program needn't handle non-finite values.
Results may differ from a plain program's by a relative error of at most 0.0003.
Values sent between devices are 32-bit elements; how exact they have to be, the bound alone decides.
A program may use at most 192 MiB of HBM per device.

v0:
```python
import math
import jax
import jax.numpy as jnp
from jax import lax
from jax.sharding import PartitionSpec as P

NSEC = 3
NODE_Z = 64
PB = 2048
SWEEPS = 3
inverse_four_pi = 1.0 / (4.0 * math.pi)


def from_behind(value, axis, by):
    count = lax.axis_size(axis)
    return lax.ppermute(value, axis, [(i, (i + by) % count) for i in range(count)])


def extended(cells, sides, width):
    for axis, dim in sides:
        count = lax.axis_size(axis)
        ends = count - 1
        head = lax.slice_in_dim(cells, 0, width, axis=dim)
        tail = lax.slice_in_dim(cells, cells.shape[dim] - width, cells.shape[dim], axis=dim)
        cells = jnp.concatenate(
            [
                lax.ppermute(tail, axis, [(i, (i + 1) % count) for i in range(ends)]),
                cells,
                lax.ppermute(head, axis, [((i + 1) % count, i) for i in range(ends)]),
            ],
            axis=dim,
        )
    return cells


def cross_three(first, second):
    return (
        first[1] * second[2] - first[2] * second[1],
        first[2] * second[0] - first[0] * second[2],
        first[0] * second[1] - first[1] * second[0],
    )


def particle_rates(place, spin, core, live, source, source_live):
    delta = [place[component][:, None] - source[component][None, :] for component in range(3)]
    spread = 0.5 * (core[:, None] * core[:, None] + source[6][None, :] * source[6][None, :])
    distance = delta[0] * delta[0] + delta[1] * delta[1] + delta[2] * delta[2] + spread
    weight = jnp.where(source_live[None, :], distance ** (-1.5), 0.0)
    steep = 3.0 * weight / distance
    source_spin = [source[3 + component][None, :] for component in range(3)]
    curl = cross_three(delta, source_spin)
    along = spin[0][:, None] * delta[0] + spin[1][:, None] * delta[1] + spin[2][:, None] * delta[2]
    velocity = jnp.stack([jnp.sum(weight * curl[component], axis=1) for component in range(3)])
    spin_sum = [jnp.sum(weight * source_spin[component], axis=1) for component in range(3)]
    bent = jnp.stack([jnp.sum(steep * along * curl[component], axis=1) for component in range(3)])
    turned = jnp.stack(cross_three(spin, spin_sum))
    factor = jnp.where(live, -inverse_four_pi, 0.0)[None, :]
    return (velocity * factor, (turned - bent) * factor)


def node_rates(points, source, source_live):
    delta = [points[component][:, None] - source[component][None, :] for component in range(3)]
    distance = (
        delta[0] * delta[0]
        + delta[1] * delta[1]
        + delta[2] * delta[2]
        + source[6][None, :] * source[6][None, :]
    )
    weight = jnp.where(source_live[None, :], distance ** (-1.5), 0.0)
    source_spin = [source[3 + component][None, :] for component in range(3)]
    curl = cross_three(delta, source_spin)
    return (
        jnp.stack([jnp.sum(weight * curl[component], axis=1) for component in range(3)])
        * -inverse_four_pi
    )


def tiled(function, arrays, count):
    tile = math.gcd(count, 256)
    pieces = count // tile

    def split_tiles(array):
        return jnp.moveaxis(array.reshape(array.shape[:-1] + (pieces, tile)), -2, 0)

    def join_tiles(array):
        moved = jnp.moveaxis(array, 0, -2)
        return moved.reshape(moved.shape[:-2] + (count,))

    results = lax.map(function, tuple((split_tiles(array) for array in arrays)))
    return jax.tree.map(join_tiles, results)


def cell_diffusion(sections, viscosity):
    total = jnp.zeros((5,) + sections.shape, jnp.float32)
    for number in range(NSEC):
        total = total + jnp.where(sections[None] == number, viscosity[number][:, None, None], 0.0)
    return total


def on_device(
    flow,
    section_map,
    viscosity,
    particle_position,
    particle_strength,
    particle_core,
    shed_counts,
    node_position,
    node_block,
):
    wake_count = lax.axis_size("wake")
    wake_index = lax.axis_index("wake")
    stops = wake_count // 2
    half = stops // 2
    slots = jnp.arange(PB, dtype=jnp.int32)
    target_count = particle_position.shape[1]
    target_slots = lax.axis_index("grid") * target_count + jnp.arange(target_count, dtype=jnp.int32)
    target_live = target_slots < shed_counts[wake_index]
    share = jnp.concatenate([particle_position, particle_strength, particle_core[None, :]], axis=0)
    block = lax.all_gather(share, "grid", axis=1, tiled=True)

    def visit(source, number, totals):
        source_live = slots < shed_counts[number]

        def visit_rates(arrays):
            return particle_rates(arrays[0], arrays[1], arrays[2], arrays[3], source, source_live)

        velocity, stretch = tiled(
            visit_rates,
            (particle_position, particle_strength, particle_core, target_live),
            target_count,
        )
        return (totals[0] + velocity, totals[1] + stretch)

    zeros = jnp.zeros((3, target_count), jnp.float32)
    first = from_behind(block, "wake", 1 - half)
    totals = visit(first, (wake_index + half - 1) % wake_count, (zeros, zeros))

    def advance(turn, carry):
        source, sums = carry
        source = from_behind(source, "wake", 1)
        return (source, visit(source, (wake_index + half - 1 - turn) % wake_count, sums))

    carried, totals = lax.fori_loop(1, stops, advance, (first, totals))
    node_count = node_position.shape[1]
    target_block = node_block[:, 0]
    capacity = 2 * node_count // wake_count
    onehot = (target_block[:, None] == jnp.arange(wake_count, dtype=jnp.int32)[None, :]).astype(
        jnp.int32
    )
    rank = jnp.sum((jnp.cumsum(onehot, axis=0) - onehot) * onehot, axis=1)
    slot = target_block * capacity + rank
    outgoing = jnp.zeros((3, wake_count * capacity), jnp.float32).at[:, slot].set(node_position)
    outgoing = outgoing.reshape(3, wake_count, capacity)
    own_live = slots < shed_counts[wake_index]
    points = lax.all_to_all(outgoing, "wake", split_axis=1, concat_axis=1, tiled=True)
    flat = points.reshape(3, -1)

    def evaluate_rates(arrays):
        return node_rates(arrays[0], block, own_live)

    result = tiled(evaluate_rates, (flat,), flat.shape[1])
    answered = result.reshape(points.shape)
    returned = lax.all_to_all(answered, "wake", split_axis=1, concat_axis=1, tiled=True)
    node_velocity = returned.reshape(3, wake_count * capacity)[:, slot]
    rows = flow.shape[1]
    columns = flow.shape[2]
    stride = columns // NODE_Z
    field = flow.at[1:4, :, ::stride].set(node_velocity.reshape(3, rows, NODE_Z))
    diffusion = cell_diffusion(section_map, viscosity)
    for sweep in range(SWEEPS):
        padded = extended(field, (("wake", 1), ("grid", 2)), 1)
        beside = (
            padded[:, 2:, 1:-1] + padded[:, :-2, 1:-1] + padded[:, 1:-1, 2:] + padded[:, 1:-1, :-2]
        )
        field = field + diffusion * (beside - 4.0 * field)
    return (field, totals[0], totals[1])


def solution(mesh):
    return jax.shard_map(
        on_device,
        mesh=mesh,
        in_specs=(
            P(None, "wake", "grid"),
            P("wake", "grid"),
            P(),
            P(None, ("wake", "grid")),
            P(None, ("wake", "grid")),
            P(("wake", "grid")),
            P(),
            P(None, ("wake", "grid")),
            P(("wake", "grid"), None),
        ),
        out_specs=(P(None, "wake", "grid"), P(None, ("wake", "grid")), P(None, ("wake", "grid"))),
        check_vma=False,
    )
```

profile of v0, /device:TPU:80, one launch (start us, length us, event | category | flops | bytes accessed | tf_op | source)
XLA Modules:
  0.0 859.3 jit_solution(195151444402644081)
XLA Ops:
  1.5 4.5 reduce-window.6
  8.8 3.3 scatter_custom_fusion
  13.0 7.3 all-to-all-start
  20.4 27.0 %all_gather.3 = f32[7,2048]{1,0:T(8,128)} all-gather(f32[7,256]{1,0:T(8,128)S(1)} %pad_maximum_fusion.33), channel_id=1, replica_groups=mesh['wake'=16,'grid'=8] {'grid'}, dimensions={1}, use_global_device_ids=true | all-gather | bytes 64512 | tf_op jit(solution)/shard_map/all_gather | solution.py:120
  49.3 42.7 %while.50 = (s32[]{:T(128)}, f32[8,3,256]{2,1,0:T(4,128)}, f32[8,3,256]{2,0,1:T(8,128)S(1)}, f32[7,2048]{1,0:T(8,128)}, f32[1,2048]{1,0:T(1,128)S(1)}, /*index=5*/s32[]{:T(128)}, s32[]{:T(128)}, s32[]{:T(128)}, s32[]{}, s32[]{}) while((s32[]{:T(128)}, f32[8,3,256]{2,1,0:T(4,128)}, f32[8,3,256]{2,0,1:T(8,128)S(1)}, ...), condition=%wide.region_8.9_spmd.clone, body=%wide.region_4.8_spmd.clone.sunk | while | flops 13110788 | bytes 179853 | solution.py:89
  51.1 2.9 fusion.113
  56.5 2.9 fusion.113
  61.8 2.9 fusion.113
  67.2 2.9 fusion.113
  72.5 2.9 fusion.113
  77.8 2.9 fusion.113
  88.5 2.9 fusion.113
  92.1 7.5 all-to-all-start.1
  99.6 20.3 %copy.69 = f32[5,16,16384]{1,2,0:T(8,128)} copy(f32[5,16,16384]{2,1,0:T(8,128)} %param.13) | data formatting | bytes 10485760
  123.6 489.6 %while.49 = (s32[]{:T(128)}, f32[5,16,16384]{1,2,0:T(8,128)}, s32[64,2]{0,1:T(2,128)S(1)}, f32[64,3,16]{2,0,1:T(8,128)S(1)}, s32[]{:T(128)}, /*index=5*/s32[3]{0:T(128)S(1)}, s32[1]{0:T(128)}, s32[]{:T(128)}) while((s32[]{:T(128)}, f32[5,16,16384]{1,2,0:T(8,128)}, s32[64,2]{0,1:T(2,128)S(1)}, f32[64,3,16]{2,0,1:T(8,128)S(1)}, s32[]{:T(128)}, ...), condition=%wide.while_cond, body=%wide.while_body.sunk | while | flops 67 | bytes 1123 | solution.py:169
  613.2 27.6 %copy.76 = f32[5,16,16384]{2,0,1:T(8,128)} copy(f32[5,16,16384]{1,2,0:T(8,128)} %get-tuple-element.407) | data formatting | bytes 10485760 | tf_op jit(solution)/shard_map/scatter | solution.py:169
  642.1 4.3 collective-permute-start.1
  649.0 4.2 collective-permute-done.1
  653.1 7.5 collective-permute-done.2
  661.6 4.7 collective-permute-start.3
  669.3 4.2 collective-permute-done.4
  673.5 17.5 %fusion.60 = f32[5,16,16384]{2,0,1:T(8,128)S(1)} fusion(f32[5,16,16384]{2,0,1:T(8,128)} %copy.76, f32[5,18,1]{2,0,1:T(8,128)S(1)} %collective-permute-done.4, f32[5,1,16384]{2,0,1:T(8,128)S(1)} %collective-permute-done.1, f32[5,1,16384]{2,0,1:T(8,128)S(1)} %collective-permute-done.2, f32[5,18,1]{2,0,1:T(8,128)S(1)} %collective-permute-done.3, ...), kind=kLoop, calls=%fused_computation.117 | loop fusion | flops 26214400 | bytes 11928332 | tf_op jit(solution)/shard_map/add | solution.py:176
  696.1 3.6 collective-permute-done.5
  699.7 7.5 collective-permute-done.6
  707.3 3.1 collective-permute-start.7
  713.5 4.0 collective-permute-done.8
  717.6 11.0 %fusion.54 = f32[5,16,16384]{2,0,1:T(8,128)S(1)} fusion(f32[5,16,16384]{2,0,1:T(8,128)S(1)} %fusion.60, f32[5,18,1]{2,0,1:T(8,128)S(1)} %collective-permute-done.8, f32[5,1,16384]{2,0,1:T(8,128)S(1)} %collective-permute-done.5, f32[5,1,16384]{2,0,1:T(8,128)S(1)} %collective-permute-done.6, f32[5,18,1]{2,0,1:T(8,128)S(1)} %collective-permute-done.7, ...), kind=kLoop, calls=%fused_computation.103 | loop fusion | flops 26214400 | bytes 11928332 | tf_op jit(solution)/shard_map/add | solution.py:176
  730.6 7.3 collective-permute-start.9
  737.9 5.0 fusion.79
  744.7 3.9 collective-permute-start.11
  750.9 4.8 collective-permute-done.12
  755.7 11.0 %fusion.48 = f32[5,16,16384]{2,0,1:T(8,128)S(1)} fusion(f32[5,16,16384]{2,0,1:T(8,128)S(1)} %fusion.54, f32[5,18,1]{2,0,1:T(8,128)S(1)} %collective-permute-done.12, f32[5,1,16384]{2,0,1:T(8,128)S(1)} %collective-permute-done.9, f32[5,1,16384]{2,0,1:T(8,128)S(1)} %collective-permute-done.10, f32[5,18,1]{2,0,1:T(8,128)S(1)} %collective-permute-done.11, ...), kind=kLoop, calls=%fused_computation.89 | loop fusion | flops 26214400 | bytes 11928332 | tf_op jit(solution)/shard_map/add | solution.py:176
  766.7 5.4 copy.77
  772.1 86.5 %while.51 = (s32[]{:T(128)}, f32[7,2048]{1,0:T(8,128)S(1)}, f32[3,256]{1,0:T(4,128)S(1)}, f32[3,256]{1,0:T(4,128)S(1)}, s32[]{:T(128)}, /*index=5*/s32[16]{0:T(1...) while((s32[]{:T(128)}, f32[7,2048]{1,0:T(8,128)S(1)}, ...), condition=%wide.region_29.30_spmd.clone, body=%wide.region_19.29_spmd.clone.sunk | while | flops 24654864 | bytes 581992 | solution.py:144
  773.9 5.5 collective-permute-done
  779.5 4.9 fusion.117
  786.3 5.5 collective-permute-done
  791.8 4.9 fusion.117
  798.7 5.5 collective-permute-done
  804.2 4.9 fusion.117
  811.1 5.5 collective-permute-done
  816.6 4.9 fusion.117
  823.5 5.5 collective-permute-done
  829.0 4.9 fusion.117
  835.8 5.5 collective-permute-done
  841.3 4.9 fusion.117
  848.2 5.5 collective-permute-done
  853.7 4.9 fusion.117
  (489 shorter events, 557.6 us)
Async XLA Ops:
  0.6 19.7 %copy-start.6 = (f32[256]{0:T(256)S(1)}, f32[256]{0:T(256)}, u32[]{:S(2)}) copy-start(f32[256]{0:T(256)} %param.18) | copy-start | bytes 3076
  0.6 19.7 %copy-start.4 = (f32[3,256]{1,0:T(4,128)S(1)}, f32[3,256]{1,0:T(4,128)}, u32[]{:S(2)}) copy-start(f32[3,256]{1,0:T(4,128)} %param.16) | copy-start | bytes 9220
  0.7 19.7 %copy-start.1 = (f32[3,256]{1,0:T(4,128)S(1)}, f32[3,256]{1,0:T(4,128)}, u32[]{:S(2)}) copy-start(f32[3,256]{1,0:T(4,128)} %param.17) | copy-start | bytes 9220
  0.7 47.6 %copy-start = (s32[16,16384]{1,0:T(8,128)S(1)}, s32[16,16384]{1,0:T(8,128)}, u32[]{:S(2)}) copy-start(s32[16,16384]{1,0:T(8,128)} %param.14) | copy-start | bytes 3145732
  8.7 39.9 %copy-start.8 = (f32[3,5]{1,0:T(4,128)S(1)}, f32[3,5]{1,0:T(4,128)}, u32[]{:S(2)}) copy-start(f32[3,5]{1,0:T(4,128)} %param.15) | copy-start | bytes 184
  8.7 40.0 %copy-start.7 = (s32[16]{0:T(128)S(1)}, s32[16]{0:T(128)}, u32[]{:S(2)}) copy-start(s32[16]{0:T(128)} %param.19) | copy-start | bytes 196
  13.0 36.3 %all-to-all-start = ((f32[3,16,128]{2,0,1:T(4,128)}), f32[3,16,128]{2,0,1:T(4,128)S(1)}, u32[]{:S(2)}, u32[]{:S(2)}) async-start(f32[3,16,128]{2,0,1:T(4,128)} %copy.62), calls=%async_computation | async-start | bytes 65536 | tf_op jit(solution)/shard_map/all_to_all | solution.py:156
  47.3 666.0 %collective-permute-start.13 = (f32[7,2048]{1,0:T(8,128)}, f32[7,2048]{1,0:T(8,128)S(1)}, u32[]{:S(2)}, u32[]{:S(2)}) collective-permute-start(f32[7,2048]{1,0:T(8,128)} %all_gather.3), channel_id=1, source_target_pairs={{0,104},{8,112},{16,120},{24,0},{32,8},{40,16},{48,24},{56,32},{64... | collective-permute-start | bytes 172040 | tf_op jit(solution)/shard_map/ppermute | solution.py:16
  92.1 27.9 %all-to-all-start.1 = ((f32[3,16,128]{2,0,1:T(4,128)}), f32[3,16,128]{2,0,1:T(4,128)S(1)}, u32[]{:S(2)}, u32[]{:S(2)}) async-start(f32[3,16,128]{2,0,1:T(4,128)} %bitcast.12), calls=%async_computation.1 | async-start | bytes 65536 | tf_op jit(solution)/shard_map/all_to_all | solution.py:164
  99.6 24.0 %copy-start.5 = (s32[3]{0:T(128)S(1)}, s32[3]{0:T(128)}, u32[]{:S(2)}) copy-start(s32[3]{0:T(128)} %constant.451) | copy-start | bytes 40
  642.1 11.0 %collective-permute-start.1 = (f32[5,1,16384]{2,0,1:T(8,128)S(1)}, f32[5,1,16384]{2,0,1:T(8,128)S(1)}, u32[]{:S(2)}, u32[]{:S(2)}) collective-permute-start(f32[5,1,16384]{2,0,1:T(8,128)S(1)} %get-tuple-element.606), channel_id=1, source_target_pairs={{8,0},{16,8},{24,16},{32,24},{40,32},{48,40},{56,48},{64,56},{72,6... | collective-permute-start | bytes 983048 | tf_op jit(solution)/shard_map/ppermute | solution.py:29
  646.5 14.2 %collective-permute-start.2 = (f32[5,1,16384]{2,0,1:T(8,128)S(1)}, f32[5,1,16384]{2,0,1:T(8,128)S(1)}, u32[]{:S(2)}, u32[]{:S(2)}) collective-permute-start(f32[5,1,16384]{2,0,1:T(8,128)S(1)} %get-tuple-element.605), channel_id=1, source_target_pairs={{0,8},{8,16},{16,24},{24,32},{32,40},{40,48},{48,56},{56,64},{64,7... | collective-permute-start | bytes 983048 | tf_op jit(solution)/shard_map/ppermute | solution.py:27
  661.6 7.7 collective-permute-start.3
  666.4 7.1 collective-permute-start.4
  691.1 8.6 %collective-permute-start.5 = (f32[5,1,16384]{2,0,1:T(8,128)S(1)}, f32[5,1,16384]{2,0,1:T(8,128)S(1)}, u32[]{:S(2)}, u32[]{:S(2)}) collective-permute-start(f32[5,1,16384]{2,0,1:T(8,128)S(1)} %get-tuple-element.604), channel_id=1, source_target_pairs={{8,0},{16,8},{24,16},{32,24},{40,32},{48,40},{56,48},{64,56},{72,6... | collective-permute-start | bytes 983048 | tf_op jit(solution)/shard_map/ppermute | solution.py:29
  693.0 14.2 %collective-permute-start.6 = (f32[5,1,16384]{2,0,1:T(8,128)S(1)}, f32[5,1,16384]{2,0,1:T(8,128)S(1)}, u32[]{:S(2)}, u32[]{:S(2)}) collective-permute-start(f32[5,1,16384]{2,0,1:T(8,128)S(1)} %get-tuple-element.603), channel_id=1, source_target_pairs={{0,8},{8,16},{16,24},{24,32},{32,40},{40,48},{48,56},{56,64},{64,7... | collective-permute-start | bytes 983048 | tf_op jit(solution)/shard_map/ppermute | solution.py:27
  707.3 6.2 collective-permute-start.7
  710.4 7.1 collective-permute-start.8
  728.7 14.2 %collective-permute-start.10 = (f32[5,1,16384]{2,0,1:T(8,128)S(1)}, f32[5,1,16384]{2,0,1:T(8,128)S(1)}, u32[]{:S(2)}, u32[]{:S(2)}) collective-permute-start(f32[5,1,16384]{2,0,1:T(8,128)S(1)} %get-tuple-element.601), channel_id=1, source_target_pairs={{0,8},{8,16},{16,24},{24,32},{32,40},{40,48},{48,56},{56,64},{64,7... | collective-permute-start | bytes 983048 | tf_op jit(solution)/shard_map/ppermute | solution.py:27
  730.6 14.0 %collective-permute-start.9 = (f32[5,1,16384]{2,0,1:T(8,128)S(1)}, f32[5,1,16384]{2,0,1:T(8,128)S(1)}, u32[]{:S(2)}, u32[]{:S(2)}) collective-permute-start(f32[5,1,16384]{2,0,1:T(8,128)S(1)} %get-tuple-element.602), channel_id=1, source_target_pairs={{8,0},{16,8},{24,16},{32,24},{40,32},{48,40},{56,48},{64,56},{72,6... | collective-permute-start | bytes 983048 | tf_op jit(solution)/shard_map/ppermute | solution.py:29
  744.7 6.2 collective-permute-start.11
  748.6 7.1 collective-permute-start.12
  772.1 7.3 collective-permute-start
  784.4 7.4 collective-permute-start
  796.8 7.4 collective-permute-start
  809.2 7.4 collective-permute-start
  821.5 7.4 collective-permute-start
  833.9 7.4 collective-permute-start
  846.3 7.4 collective-permute-start
  858.7 0.6 copy-start.2
  858.7 0.6 copy-start.3
where the time goes:
time: 872 us; the launch traced here: 859 us
  other arithmetic  422 us (48%)
  local copies, waits for them, and re-layouts  277 us (32%)
  waiting for transfers between devices  76.8 us (9%)
  starting transfers between devices  54.1 us (6%)
  blocking collectives  27 us (3%)
    scatter x128, other arithmetic  291 us
    scatter x192, local copies, waits for them, and re-layouts  198 us
    add x3, other arithmetic, on_device(): field = field + diffusion * (beside - 4.0 * field)  39.5 us
    reduce_sum x8, other arithmetic, particle_rates(): jnp.sum(steep * along * curl[component], axis=1)  39.1 us
    ppermute x8, waiting for transfers between devices, from_behind(): lax.ppermute(value, axis, [(i, (i + by) % count) for i in range(count)])  38.3 us
    ppermute x6, waiting for transfers between devices, extended(): lax.ppermute(tail, axis, [(i, (i + 1) % count) for i in range(ends)])  28.1 us
    scatter x1, local copies, waits for them, and re-layouts, on_device(): flow.at[1:4, :, ::stride].set(node_velocity.reshape(3, rows, NODE_Z))  27.6 us
    unnamed x21, local copies, waits for them, and re-layouts  27.3 us
  transfers between devices with their start and end apart: 22, of which 18 were waited for; matrix products, arithmetic and copies ran while one was open for 73% of the time, Pallas kernels for 0%

commit v1 on v0

--- a/solution.py
+++ b/solution.py
@@ -117,7 +117,9 @@
     target_slots = lax.axis_index("grid") * target_count + jnp.arange(target_count, dtype=jnp.int32)
     target_live = target_slots < shed_counts[wake_index]
     share = jnp.concatenate([particle_position, particle_strength, particle_core[None, :]], axis=0)
-    block = lax.all_gather(share, "grid", axis=1, tiled=True)
+    block = jnp.concatenate(
+        lax.all_to_all(jnp.stack([share] * lax.axis_size("grid")), "grid", 0, 0), axis=1
+    )
 
     def visit(source, number, totals):
         source_live = slots < shed_counts[number]

time: 872 us -> 845 us (0.969)
  blocking collectives: 27 us -> 0 us
    all_gather x1 -> x0, blocking collectives: 27 us -> none  [on_device(): block = lax.all_gather(share, 'grid', axis=1, tiled=True)]
  transfers between devices with their start and end apart: 22 -> 23, of which waited for: 18 -> 21; matrix products, arithmetic and copies ran while one was open for 73% -> 5% of each run, Pallas kernels for 0% -> 0%
where the time goes in v1:
time: 845 us; the launch traced here: 833 us
  other arithmetic  421 us (50%)
  local copies, waits for them, and re-layouts  269 us (32%)
  waiting for transfers between devices  83.9 us (10%)
  starting transfers between devices  56.7 us (7%)
    scatter x128, other arithmetic  291 us
    scatter x192, local copies, waits for them, and re-layouts  198 us
    add x3, other arithmetic, on_device(): field = field + diffusion * (beside - 4.0 * field)  39.5 us
    reduce_sum x8, other arithmetic, particle_rates(): jnp.sum(steep * along * curl[component], axis=1)  39.1 us
    ppermute x8, waiting for transfers between devices, from_behind(): lax.ppermute(value, axis, [(i, (i + by) % count) for i in range(count)])  38.4 us
    scatter x1, local copies, waits for them, and re-layouts, on_device(): flow.at[1:4, :, ::stride].set(node_velocity.reshape(3, rows, NODE_Z))  27.6 us
    unnamed x21, local copies, waits for them, and re-layouts  27.3 us
    ppermute x6, waiting for transfers between devices, extended(): lax.ppermute(tail, axis, [(i, (i + 1) % count) for i in range(ends)])  27 us
  transfers between devices with their start and end apart: 23, of which 21 were waited for; matrix products, arithmetic and copies ran while one was open for 5% of the time, Pallas kernels for 0%

profile of v1, /device:TPU:80, one launch (start us, length us, event | category | flops | bytes accessed | tf_op | source)
XLA Modules:
  0.0 832.8 jit_solution(18131838848933984130)
XLA Ops:
  1.4 4.5 reduce-window.6
  8.8 3.3 scatter_custom_fusion
  13.0 7.3 all-to-all-start
  20.8 4.3 all-to-all-done
  25.7 5.7 all-to-all-start.1
  32.1 3.4 all-to-all-done.1
  35.5 33.8 %while.50 = (s32[]{:T(128)}, f32[8,3,256]{2,1,0:T(4,128)}, f32[8,3,256]{2,0,1:T(8,128)S(1)}, f32[7,2048]{1,0:T(8,128)S(1)}, f32[1,2048]{1,0:T(1,128)S(1)}, /*index=5*/s32[]{:T(128)}, s32[]{:T(128)}, s32[]{:T(128)}, s32[]{}, s32[]{}) while((s32[]{:T(128)}, f32[8,3,256]{2,1,0:T(4,128)}, f32[8,3,256]{2,0,1:T(8,128)S(1)}, ...), condition=%wide.region_8.9_spmd.clone, body=%wide.region_4.8_spmd.clone.sunk | while | flops 13110788 | bytes 179853 | solution.py:89
  36.2 2.9 fusion.113
  40.4 2.9 fusion.113
  44.7 2.9 fusion.113
  48.9 2.9 fusion.113
  57.3 2.9 fusion.113
  65.8 2.9 fusion.113
  69.3 5.6 all-to-all-start.2
  75.0 20.3 %copy.69 = f32[5,16,16384]{1,2,0:T(8,128)} copy(f32[5,16,16384]{2,1,0:T(8,128)} %param.13) | data formatting | bytes 10485760
  99.0 489.6 %while.49 = (s32[]{:T(128)}, f32[5,16,16384]{1,2,0:T(8,128)}, s32[64,2]{0,1:T(2,128)S(1)}, f32[64,3,16]{2,0,1:T(8,128)S(1)}, s32[]{:T(128)}, /*index=5*/s32[3]{0:T(128)S(1)}, s32[1]{0:T(128)}, s32[]{:T(128)}) while((s32[]{:T(128)}, f32[5,16,16384]{1,2,0:T(8,128)}, s32[64,2]{0,1:T(2,128)S(1)}, f32[64,3,16]{2,0,1:T(8,128)S(1)}, s32[]{:T(128)}, ...), condition=%wide.while_cond, body=%wide.while_body.sunk | while | flops 67 | bytes 1123 | solution.py:171
  588.6 27.6 %copy.76 = f32[5,16,16384]{2,0,1:T(8,128)} copy(f32[5,16,16384]{1,2,0:T(8,128)} %get-tuple-element.407) | data formatting | bytes 10485760 | tf_op jit(solution)/shard_map/scatter | solution.py:171
  617.5 4.3 collective-permute-start.1
  624.5 4.0 collective-permute-done.1
  628.5 7.5 collective-permute-done.2
  637.0 4.1 collective-permute-start.3
  643.3 5.0 collective-permute-done.4
  648.2 17.5 %fusion.60 = f32[5,16,16384]{2,0,1:T(8,128)S(1)} fusion(f32[5,16,16384]{2,0,1:T(8,128)} %copy.76, f32[5,18,1]{2,0,1:T(8,128)S(1)} %collective-permute-done.4, f32[5,1,16384]{2,0,1:T(8,128)S(1)} %collective-permute-done.1, f32[5,1,16384]{2,0,1:T(8,128)S(1)} %collective-permute-done.2, f32[5,18,1]{2,0,1:T(8,128)S(1)} %collective-permute-done.3, ...), kind=kLoop, calls=%fused_computation.117 | loop fusion | flops 26214400 | bytes 11928332 | tf_op jit(solution)/shard_map/add | solution.py:178
  670.8 4.3 collective-permute-done.5
  675.1 6.8 collective-permute-done.6
  683.9 4.1 collective-permute-start.8
  691.1 11.1 %fusion.54 = f32[5,16,16384]{2,0,1:T(8,128)S(1)} fusion(f32[5,16,16384]{2,0,1:T(8,128)S(1)} %fusion.60, f32[5,18,1]{2,0,1:T(8,128)S(1)} %collective-permute-done.8, f32[5,1,16384]{2,0,1:T(8,128)S(1)} %collective-permute-done.5, f32[5,1,16384]{2,0,1:T(8,128)S(1)} %collective-permute-done.6, f32[5,18,1]{2,0,1:T(8,128)S(1)} %collective-permute-done.7, ...), kind=kLoop, calls=%fused_computation.103 | loop fusion | flops 26214400 | bytes 11928332 | tf_op jit(solution)/shard_map/add | solution.py:178
  704.2 7.3 collective-permute-start.9
  711.4 4.9 fusion.79
  718.2 3.9 collective-permute-start.11
  724.5 4.8 collective-permute-done.12
  729.3 11.0 %fusion.48 = f32[5,16,16384]{2,0,1:T(8,128)S(1)} fusion(f32[5,16,16384]{2,0,1:T(8,128)S(1)} %fusion.54, f32[5,18,1]{2,0,1:T(8,128)S(1)} %collective-permute-done.12, f32[5,1,16384]{2,0,1:T(8,128)S(1)} %collective-permute-done.9, f32[5,1,16384]{2,0,1:T(8,128)S(1)} %collective-permute-done.10, f32[5,18,1]{2,0,1:T(8,128)S(1)} %collective-permute-done.11, ...), kind=kLoop, calls=%fused_computation.89 | loop fusion | flops 26214400 | bytes 11928332 | tf_op jit(solution)/shard_map/add | solution.py:178
  740.3 5.4 copy.77
  745.7 86.5 %while.51 = (s32[]{:T(128)}, f32[7,2048]{1,0:T(8,128)S(1)}, f32[3,256]{1,0:T(4,128)S(1)}, f32[3,256]{1,0:T(4,128)S(1)}, s32[]{:T(128)}, /*index=5*/s32[16]{0:T(1...) while((s32[]{:T(128)}, f32[7,2048]{1,0:T(8,128)S(1)}, ...), condition=%wide.region_29.30_spmd.clone, body=%wide.region_19.29_spmd.clone.sunk | while | flops 24654864 | bytes 581992 | solution.py:146
  747.5 5.5 collective-permute-done
  753.0 4.9 fusion.117
  759.9 5.5 collective-permute-done
  765.4 4.9 fusion.117
  772.3 5.5 collective-permute-done
  777.8 4.9 fusion.117
  784.6 5.5 collective-permute-done
  790.2 4.9 fusion.117
  797.0 5.5 collective-permute-done
  802.5 4.9 fusion.117
  809.4 5.5 collective-permute-done
  814.9 4.9 fusion.117
  821.7 5.5 collective-permute-done
  827.3 4.9 fusion.117
  (491 shorter events, 552.5 us)
Async XLA Ops:
  0.6 19.7 %copy-start = (s32[16,16384]{1,0:T(8,128)S(1)}, s32[16,16384]{1,0:T(8,128)}, u32[]{:S(2)}) copy-start(s32[16,16384]{1,0:T(8,128)} %param.14) | copy-start | bytes 3145732
  8.7 12.1 %copy-start.1 = (f32[3,256]{1,0:T(4,128)S(1)}, f32[3,256]{1,0:T(4,128)}, u32[]{:S(2)}) copy-start(f32[3,256]{1,0:T(4,128)} %param.17) | copy-start | bytes 9220
  8.7 12.1 %copy-start.4 = (f32[3,256]{1,0:T(4,128)S(1)}, f32[3,256]{1,0:T(4,128)}, u32[]{:S(2)}) copy-start(f32[3,256]{1,0:T(4,128)} %param.16) | copy-start | bytes 9220
  8.7 12.1 %copy-start.6 = (f32[256]{0:T(256)S(1)}, f32[256]{0:T(256)}, u32[]{:S(2)}) copy-start(f32[256]{0:T(256)} %param.18) | copy-start | bytes 3076
  8.7 22.7 %copy-start.8 = (f32[3,5]{1,0:T(4,128)S(1)}, f32[3,5]{1,0:T(4,128)}, u32[]{:S(2)}) copy-start(f32[3,5]{1,0:T(4,128)} %param.15) | copy-start | bytes 184
  8.7 22.7 %copy-start.7 = (s32[16]{0:T(128)S(1)}, s32[16]{0:T(128)}, u32[]{:S(2)}) copy-start(s32[16]{0:T(128)} %param.19) | copy-start | bytes 196
  13.0 12.1 %all-to-all-start = ((f32[3,16,128]{2,0,1:T(4,128)}), f32[3,16,128]{2,0,1:T(4,128)S(1)}, u32[]{:S(2)}, u32[]{:S(2)}) async-start(f32[3,16,128]{2,0,1:T(4,128)} %copy.62), calls=%async_computation | async-start | bytes 65536 | tf_op jit(solution)/shard_map/all_to_all | solution.py:158
  25.7 9.8 %all-to-all-start.1 = ((f32[8,7,256]{2,1,0:T(8,128)}), f32[8,7,256]{2,1,0:T(8,128)S(1)}, u32[]{:S(2)}, u32[]{:S(2)}) async-start(f32[8,7,256]{2,1,0:T(8,128)} %stack.131), calls=%async_computation.1 | async-start | bytes 131072 | tf_op jit(solution)/shard_map/all_to_all | solution.py:121
  69.3 26.0 %all-to-all-start.2 = ((f32[3,16,128]{2,0,1:T(4,128)}), f32[3,16,128]{2,0,1:T(4,128)S(1)}, u32[]{:S(2)}, u32[]{:S(2)}) async-start(f32[3,16,128]{2,0,1:T(4,128)} %bitcast.15), calls=%async_computation.2 | async-start | bytes 65536 | tf_op jit(solution)/shard_map/all_to_all | solution.py:166
  75.0 24.0 %copy-start.5 = (s32[3]{0:T(128)S(1)}, s32[3]{0:T(128)}, u32[]{:S(2)}) copy-start(s32[3]{0:T(128)} %constant.451) | copy-start | bytes 40
  617.5 11.0 %collective-permute-start.1 = (f32[5,1,16384]{2,0,1:T(8,128)S(1)}, f32[5,1,16384]{2,0,1:T(8,128)S(1)}, u32[]{:S(2)}, u32[]{:S(2)}) collective-permute-start(f32[5,1,16384]{2,0,1:T(8,128)S(1)} %get-tuple-element.606), channel_id=1, source_target_pairs={{8,0},{16,8},{24,16},{32,24},{40,32},{48,40},{56,48},{64,56},{72,6... | collective-permute-start | bytes 983048 | tf_op jit(solution)/shard_map/ppermute | solution.py:29
  621.8 14.2 %collective-permute-start.2 = (f32[5,1,16384]{2,0,1:T(8,128)S(1)}, f32[5,1,16384]{2,0,1:T(8,128)S(1)}, u32[]{:S(2)}, u32[]{:S(2)}) collective-permute-start(f32[5,1,16384]{2,0,1:T(8,128)S(1)} %get-tuple-element.605), channel_id=1, source_target_pairs={{0,8},{8,16},{16,24},{24,32},{32,40},{40,48},{48,56},{56,64},{64,7... | collective-permute-start | bytes 983048 | tf_op jit(solution)/shard_map/ppermute | solution.py:27
  637.0 6.2 collective-permute-start.3
  641.1 7.1 collective-permute-start.4
  665.8 9.3 %collective-permute-start.5 = (f32[5,1,16384]{2,0,1:T(8,128)S(1)}, f32[5,1,16384]{2,0,1:T(8,128)S(1)}, u32[]{:S(2)}, u32[]{:S(2)}) collective-permute-start(f32[5,1,16384]{2,0,1:T(8,128)S(1)} %get-tuple-element.604), channel_id=1, source_target_pairs={{8,0},{16,8},{24,16},{32,24},{40,32},{48,40},{56,48},{64,56},{72,6... | collective-permute-start | bytes 983048 | tf_op jit(solution)/shard_map/ppermute | solution.py:29
  667.7 14.2 %collective-permute-start.6 = (f32[5,1,16384]{2,0,1:T(8,128)S(1)}, f32[5,1,16384]{2,0,1:T(8,128)S(1)}, u32[]{:S(2)}, u32[]{:S(2)}) collective-permute-start(f32[5,1,16384]{2,0,1:T(8,128)S(1)} %get-tuple-element.603), channel_id=1, source_target_pairs={{0,8},{8,16},{16,24},{24,32},{32,40},{40,48},{48,56},{56,64},{64,7... | collective-permute-start | bytes 983048 | tf_op jit(solution)/shard_map/ppermute | solution.py:27
  670.7 17.3 %collective-permute-start.13 = (f32[7,2048]{1,0:T(8,128)S(1)}, f32[7,2048]{1,0:T(8,128)S(1)}, u32[]{:S(2)}, u32[]{:S(2)}) collective-permute-start(f32[7,2048]{1,0:T(8,128)S(1)} %get-tuple-element.951), channel_id=1, source_target_pairs={{0,104},{8,112},{16,120},{24,0},{32,8},{40,16},{48,24},{56,32},{64... | collective-permute-start | bytes 172040 | tf_op jit(solution)/shard_map/ppermute | solution.py:16
  682.0 6.2 collective-permute-start.7
  683.9 7.1 collective-permute-start.8
  702.2 14.2 %collective-permute-start.10 = (f32[5,1,16384]{2,0,1:T(8,128)S(1)}, f32[5,1,16384]{2,0,1:T(8,128)S(1)}, u32[]{:S(2)}, u32[]{:S(2)}) collective-permute-start(f32[5,1,16384]{2,0,1:T(8,128)S(1)} %get-tuple-element.601), channel_id=1, source_target_pairs={{0,8},{8,16},{16,24},{24,32},{32,40},{40,48},{48,56},{56,64},{64,7... | collective-permute-start | bytes 983048 | tf_op jit(solution)/shard_map/ppermute | solution.py:27
  704.2 14.0 %collective-permute-start.9 = (f32[5,1,16384]{2,0,1:T(8,128)S(1)}, f32[5,1,16384]{2,0,1:T(8,128)S(1)}, u32[]{:S(2)}, u32[]{:S(2)}) collective-permute-start(f32[5,1,16384]{2,0,1:T(8,128)S(1)} %get-tuple-element.602), channel_id=1, source_target_pairs={{8,0},{16,8},{24,16},{32,24},{40,32},{48,40},{56,48},{64,56},{72,6... | collective-permute-start | bytes 983048 | tf_op jit(solution)/shard_map/ppermute | solution.py:29
  718.2 6.2 collective-permute-start.11
  722.1 7.1 collective-permute-start.12
  745.7 7.3 collective-permute-start
  758.0 7.4 collective-permute-start
  770.4 7.4 collective-permute-start
  782.7 7.4 collective-permute-start
  795.1 7.4 collective-permute-start
  807.5 7.4 collective-permute-start
  819.9 7.4 collective-permute-start
  832.2 0.6 copy-start.2
  832.2 0.6 copy-start.3
